TPU v7x, 32 devices: a whole 2x2x4 slice. The times are simulated.
32 devices in a mesh: dp: 4 (over y, x), expert: 8 (over z, core).
Axes of the slice: x: 2, y: 2, z: 4, core: 2. Of those that a mesh axis runs over, the one named last changes fastest.
Arguments:
- layer_input: bfloat16 [6144, 2048], P(('dp', 'expert')), may hold values from -6 to 6
- out_cotangent: bfloat16 [6144, 2048], P(('dp', 'expert')), may hold values from -6 to 6
- segments: int32 [32, 192], P(('dp', 'expert')), may hold values from 0 to 2, never falling along the last dimension, each value on 1 to 96 neighbouring positions
- routes: int32 [6144, 8], P(('dp', 'expert')), may hold values from 0 to 23, all different within a row; in each aligned block of 192 rows (0 to 191, 192 to 383, ...) at most 72 rows name the same one
- w_qkv: bfloat16 [2048, 6144], P(('dp', 'expert')), may hold values from -0.125 to 0.125
- w_out: bfloat16 [2048, 2048], P(('dp', 'expert')), may hold values from -0.5 to 0.5
- w_router: bfloat16 [2048, 24], P(('dp', 'expert')), may hold values from -0.0625 to 0.0625
- attn_gain: bfloat16 [2048], P(('dp', 'expert')), may hold values from 0.5 to 1.5
- mlp_gain: bfloat16 [2048], P(('dp', 'expert')), may hold values from 0.5 to 1.5
- query_gain: bfloat16 [2048], P(('dp', 'expert')), may hold values from 0.099609375 to 1.8984375
- key_gain: bfloat16 [2048], P(('dp', 'expert')), may hold values from 0.099609375 to 1.8984375
- w_gate_up: bfloat16 [24, 2048, 2048], P('expert'), may hold values from -0.125 to 0.125
- w_down: bfloat16 [24, 1024, 2048], P('expert'), may hold values from -0.75 to 0.75
Outputs:
- out: bfloat16 [6144, 2048], P(('dp', 'expert'))
- grad_input: float32 [6144, 2048], P(('dp', 'expert'))
- grad_qkv: float32 [2048, 3, 2048], P('dp', None, 'expert')
- grad_out: float32 [2048, 2048], P('expert', 'dp')
- grad_router: float32 [2048, 24], P(('dp', 'expert'))
- grad_attn_gain: float32 [2048], P(('dp', 'expert'))
- grad_mlp_gain: float32 [2048], P(('dp', 'expert'))
- grad_query_gain: float32 [2048], P('expert')
- grad_key_gain: float32 [2048], P('expert')
- grad_gate_up: float32 [24, 2048, 2048], P('expert', 'dp')
- grad_down: float32 [24, 1024, 2048], P('expert', 'dp')
Inputs may be any that keep to these rules, and one draw needn't show every extreme that they name: `routes`: each row names 8 different experts. Among the rows of one device no expert is named more than 72 times, a bound that some block reaches. `segments`: within a sequence the numbers never fall; a document has at most 96 tokens and one has exactly that many.
All inputs are finite; a program needn't handle non-finite values.
Results may differ from a plain program's by a relative error of at most 0.02.
Values may be sent and summed in bfloat16 or wider, within the bound.
A program may use at most 320 MiB of HBM per device.

v0:
```python
import math
import jax
import jax.numpy as jnp
from jax import lax
from jax.sharding import PartitionSpec as P

HEADS = 16
NORM_EPS = 1e-05


def rms_scale(values):
    return lax.rsqrt(jnp.mean(values * values, axis=-1, keepdims=True) + NORM_EPS)


def rotary(values, direction):
    length = values.shape[-3]
    half_size = values.shape[-1] // 2
    index_half = jnp.arange(half_size, dtype=jnp.float32)
    frequency = jnp.exp(index_half * (-2.0 * math.log(10000.0) / values.shape[-1]))
    angles = jnp.arange(length, dtype=jnp.float32)[:, None] * frequency[None, :]
    cosine = jnp.cos(angles)[:, None, :]
    sine_table = direction * jnp.sin(angles)[:, None, :]
    first_half = values[..., :half_size]
    second = values[..., half_size:]
    return jnp.concatenate(
        [first_half * cosine - second * sine_table, second * cosine + first_half * sine_table],
        axis=-1,
    )


def norm_back(grad_normed, normed, scale_rows):
    return scale_rows * (
        grad_normed - normed * jnp.mean(grad_normed * normed, axis=-1, keepdims=True)
    )


def contract_rows(left_side, right_side):
    return lax.dot_general(
        left_side, right_side, (((0,), (0,)), ((), ())), preferred_element_type=jnp.float32
    )


def contract_cols(left_side, right_side):
    return lax.dot_general(
        left_side, right_side, (((1,), (1,)), ((), ())), preferred_element_type=jnp.float32
    )


def masked_scores(query_rot, key_rot, allowed, scaling):
    raw_scores = (
        jnp.einsum("gqhd,gkhd->ghqk", query_rot, key_rot, preferred_element_type=jnp.float32)
        * scaling
    )
    return jnp.where(allowed[:, None], raw_scores, -1e30)


def on_device(
    layer_input,
    out_cotangent,
    segments,
    routes,
    w_qkv,
    w_out,
    w_router,
    attn_gain,
    mlp_gain,
    query_gain,
    key_gain,
    w_gate_up,
    w_down,
):
    row_count, model_dim = layer_input.shape
    top_count = routes.shape[1]
    expert_count = w_router.shape[1]
    head_size = model_dim // HEADS
    capacity = (row_count * top_count * 9 // 8 + expert_count - 1) // expert_count
    slot_count = expert_count * capacity
    scaling = 1.0 / math.sqrt(head_size)
    dp_count = lax.axis_size("dp")
    dense = (w_qkv, w_out, w_router, attn_gain, mlp_gain, query_gain, key_gain)
    qkv_full, out_full, router_full, gain_attn, gain_mlp, gain_query, gain_key = (
        lax.all_gather(dense[0], ("dp", "expert"), axis=0, tiled=True),
        lax.all_gather(dense[1], ("dp", "expert"), axis=0, tiled=True),
        lax.all_gather(dense[2], ("dp", "expert"), axis=0, tiled=True),
        lax.all_gather(dense[3], ("dp", "expert"), axis=0, tiled=True),
        lax.all_gather(dense[4], ("dp", "expert"), axis=0, tiled=True),
        lax.all_gather(dense[5], ("dp", "expert"), axis=0, tiled=True),
        lax.all_gather(dense[6], ("dp", "expert"), axis=0, tiled=True),
    )
    gain_attn = gain_attn.astype(jnp.float32)
    gain_mlp = gain_mlp.astype(jnp.float32)
    gain_query = gain_query.astype(jnp.float32)
    gain_key = gain_key.astype(jnp.float32)
    inputs = layer_input.astype(jnp.float32)
    scale_attn = rms_scale(inputs)
    normed_attn = inputs * scale_attn
    hidden_one = (normed_attn * gain_attn).astype(jnp.bfloat16)
    group_count = segments.shape[0]
    heads_here = model_dim // head_size
    projected = jnp.dot(hidden_one, qkv_full, preferred_element_type=jnp.float32)
    query_rows = projected[:, :model_dim]
    key_rows = projected[:, model_dim : 2 * model_dim]
    value_rows = projected[:, 2 * model_dim :]
    square_query = jnp.sum(query_rows * query_rows, axis=-1, keepdims=True)
    square_key = jnp.sum(key_rows * key_rows, axis=-1, keepdims=True)
    scale_query = lax.rsqrt(square_query / model_dim + NORM_EPS)
    scale_key = lax.rsqrt(square_key / model_dim + NORM_EPS)
    normed_query = query_rows * scale_query
    normed_key = key_rows * scale_key
    head_shape = (group_count, row_count, heads_here, head_size)
    query_rot = rotary((normed_query * gain_query).reshape(head_shape), 1.0).astype(jnp.bfloat16)
    key_rot = rotary((normed_key * gain_key).reshape(head_shape), 1.0).astype(jnp.bfloat16)
    value_low = value_rows.reshape(head_shape).astype(jnp.bfloat16)
    position = jnp.arange(row_count)
    allowed = (position[:, None] >= position[None, :])[None] & (
        segments[:, :, None] == segments[:, None, :]
    )
    scores = masked_scores(query_rot, key_rot, allowed, scaling)
    row_top = jnp.max(scores, axis=-1, keepdims=True)
    expanded = jnp.exp(scores - row_top)
    row_total = jnp.sum(expanded, axis=-1, keepdims=True)
    log_total = row_top + jnp.log(row_total)
    attn_low = (expanded / row_total).astype(jnp.bfloat16)
    attended = jnp.einsum(
        "ghqk,gkhd->gqhd", attn_low, value_low, preferred_element_type=jnp.float32
    )
    attended = attended.reshape(group_count * row_count, model_dim).astype(jnp.bfloat16)
    attn_proj = jnp.dot(attended, out_full, preferred_element_type=jnp.float32)
    residual = inputs + attn_proj
    scale_mlp = rms_scale(residual)
    normed_mlp = residual * scale_mlp
    hidden_two = (normed_mlp * gain_mlp).astype(jnp.bfloat16)
    logits = jnp.dot(hidden_two, router_full, preferred_element_type=jnp.float32)
    chooser = (routes[:, :, None] == jnp.arange(expert_count)[None, None, :]).astype(jnp.float32)
    chosen = jnp.sum(chooser * logits[:, None, :], axis=-1)
    gate_values = jax.nn.softmax(chosen, axis=-1)
    used_table = jnp.sum(chooser, axis=1).astype(jnp.bfloat16)
    lower_tri = (position[:, None] > position[None, :]).astype(jnp.bfloat16)
    earlier = jnp.dot(lower_tri, used_table, preferred_element_type=jnp.float32)
    rank_in = jnp.sum(chooser * earlier[:, None, :], axis=-1).astype(jnp.int32)
    slot_index = routes * capacity + rank_in
    slot_flat = slot_index.reshape(-1)
    dispatch_table = jnp.any(
        slot_index[None, :, :] == jnp.arange(slot_count)[:, None, None], axis=-1
    ).astype(jnp.bfloat16)
    send_rows = jnp.dot(dispatch_table, hidden_two, preferred_element_type=jnp.float32).astype(
        jnp.bfloat16
    )
    send_rows = send_rows.reshape(expert_count, capacity, model_dim)
    expert_rows = lax.all_to_all(send_rows, "expert", split_axis=0, concat_axis=1, tiled=True)
    hidden = jnp.einsum("erd,edf->erf", expert_rows, w_gate_up, preferred_element_type=jnp.float32)
    hidden_size = hidden.shape[2] // 2
    gate_part = hidden[..., :hidden_size]
    up_part = hidden[..., hidden_size:]
    sigmoid_gate = jax.nn.sigmoid(gate_part)
    silu_gate = gate_part * sigmoid_gate
    activated = (silu_gate * up_part).astype(jnp.bfloat16)
    expert_out = jnp.einsum(
        "erf,efd->erd", activated, w_down, preferred_element_type=jnp.float32
    ).astype(jnp.bfloat16)
    returned = lax.all_to_all(
        expert_out, "expert", split_axis=1, concat_axis=0, tiled=True
    ).reshape(slot_count, model_dim)
    picked = (
        jnp.take(returned, slot_flat, axis=0)
        .reshape(row_count, top_count, model_dim)
        .astype(jnp.float32)
    )
    mixture = jnp.sum(gate_values[:, :, None] * picked, axis=1)
    output = (residual + mixture).astype(jnp.bfloat16)
    grad_out_rows = out_cotangent.astype(jnp.float32)
    grad_gates = jnp.sum(picked * grad_out_rows[:, None, :], axis=-1)
    grad_slots = (
        (gate_values[:, :, None] * grad_out_rows[:, None, :])
        .astype(jnp.bfloat16)
        .reshape(row_count * top_count, model_dim)
    )
    back_send = jnp.zeros((slot_count, model_dim), jnp.bfloat16).at[slot_flat].set(grad_slots)
    back_send = back_send.reshape(expert_count, capacity, model_dim)
    grad_expert_out = lax.all_to_all(back_send, "expert", split_axis=0, concat_axis=1, tiled=True)
    grad_act = jnp.einsum(
        "erd,efd->erf", grad_expert_out, w_down, preferred_element_type=jnp.float32
    )
    grad_w_down = jnp.einsum(
        "erf,erd->efd", activated, grad_expert_out, preferred_element_type=jnp.float32
    )
    grad_gate = grad_act * up_part * sigmoid_gate * (1.0 + gate_part * (1.0 - sigmoid_gate))
    grad_up = grad_act * silu_gate
    grad_hidden = jnp.concatenate([grad_gate, grad_up], axis=-1).astype(jnp.bfloat16)
    grad_w_gate_up = jnp.einsum(
        "erd,erf->edf", expert_rows, grad_hidden, preferred_element_type=jnp.float32
    )
    grad_rows = jnp.einsum(
        "erf,edf->erd", grad_hidden, w_gate_up, preferred_element_type=jnp.float32
    ).astype(jnp.bfloat16)
    grad_back = lax.all_to_all(
        grad_rows, "expert", split_axis=1, concat_axis=0, tiled=True
    ).reshape(slot_count, model_dim)
    grad_two = contract_rows(dispatch_table, grad_back)
    grad_chosen = gate_values * (
        grad_gates - jnp.sum(gate_values * grad_gates, axis=-1, keepdims=True)
    )
    grad_logits = jnp.sum(chooser * grad_chosen[:, :, None], axis=1).astype(jnp.bfloat16)
    grad_router = contract_rows(hidden_two, grad_logits)
    grad_two = grad_two + contract_cols(grad_logits, router_full)
    grad_gain_mlp = jnp.sum(grad_two * normed_mlp, axis=0)
    grad_resid = grad_out_rows + norm_back(grad_two * gain_mlp, normed_mlp, scale_mlp)
    grad_attn = grad_resid.astype(jnp.bfloat16)
    grad_w_out = contract_rows(attended, grad_attn)
    grad_attended = contract_cols(grad_attn, out_full).astype(jnp.bfloat16).reshape(head_shape)
    attn_again = jnp.exp(masked_scores(query_rot, key_rot, allowed, scaling) - log_total)
    attn_again_low = attn_again.astype(jnp.bfloat16)
    grad_value = jnp.einsum(
        "ghqk,gqhd->gkhd", attn_again_low, grad_attended, preferred_element_type=jnp.float32
    )
    grad_attn_weights = jnp.einsum(
        "gqhd,gkhd->ghqk", grad_attended, value_low, preferred_element_type=jnp.float32
    )
    row_delta = jnp.sum(grad_attn_weights * attn_again, axis=-1, keepdims=True)
    grad_scores = (attn_again * (grad_attn_weights - row_delta)).astype(jnp.bfloat16)
    grad_query_rot = (
        jnp.einsum("ghqk,gkhd->gqhd", grad_scores, key_rot, preferred_element_type=jnp.float32)
        * scaling
    )
    grad_key_rot = (
        jnp.einsum("ghqk,gqhd->gkhd", grad_scores, query_rot, preferred_element_type=jnp.float32)
        * scaling
    )
    grad_query_normed = rotary(grad_query_rot, -1.0).reshape(group_count * row_count, model_dim)
    grad_key_normed = rotary(grad_key_rot, -1.0).reshape(group_count * row_count, model_dim)
    grad_gain_query = jnp.sum(grad_query_normed * normed_query, axis=0)
    grad_gain_key = jnp.sum(grad_key_normed * normed_key, axis=0)
    weighted_query = grad_query_normed * gain_query
    weighted_key = grad_key_normed * gain_key
    dot_query = jnp.sum(weighted_query * normed_query, axis=-1, keepdims=True)
    dot_key = jnp.sum(weighted_key * normed_key, axis=-1, keepdims=True)
    grad_query = scale_query * (weighted_query - normed_query * (dot_query / model_dim))
    grad_key = scale_key * (weighted_key - normed_key * (dot_key / model_dim))
    grad_proj = jnp.concatenate(
        [grad_query, grad_key, grad_value.reshape(group_count * row_count, model_dim)], axis=-1
    ).astype(jnp.bfloat16)
    grad_w_qkv = contract_rows(hidden_one, grad_proj).reshape(model_dim, 3, model_dim)
    grad_one = contract_cols(grad_proj, qkv_full)
    grad_gain_attn = jnp.sum(grad_one * normed_attn, axis=0)
    grad_inputs = grad_resid + norm_back(grad_one * gain_attn, normed_attn, scale_attn)
    gain_pair = jnp.stack([grad_gain_query, grad_gain_key])
    head_qkv, head_out, head_gains = (
        lax.psum_scatter(
            grad_w_qkv.astype(jnp.bfloat16), "expert", scatter_dimension=2, tiled=True
        ).astype(jnp.float32),
        lax.psum_scatter(
            grad_w_out.astype(jnp.bfloat16), "expert", scatter_dimension=0, tiled=True
        ).astype(jnp.float32),
        lax.psum_scatter(
            gain_pair.astype(jnp.bfloat16), "expert", scatter_dimension=1, tiled=True
        ).astype(jnp.float32),
    )
    spread_gains = jnp.broadcast_to(head_gains[None], (dp_count,) + head_gains.shape)
    summed = (
        lax.psum_scatter(
            head_qkv.astype(jnp.bfloat16), "dp", scatter_dimension=0, tiled=True
        ).astype(jnp.float32),
        lax.psum_scatter(
            head_out.astype(jnp.bfloat16), "dp", scatter_dimension=1, tiled=True
        ).astype(jnp.float32),
        lax.psum_scatter(
            spread_gains.astype(jnp.bfloat16), "dp", scatter_dimension=0, tiled=True
        ).astype(jnp.float32),
        lax.psum_scatter(
            grad_w_gate_up.astype(jnp.bfloat16), "dp", scatter_dimension=1, tiled=True
        ).astype(jnp.float32),
        lax.psum_scatter(
            grad_w_down.astype(jnp.bfloat16), "dp", scatter_dimension=1, tiled=True
        ).astype(jnp.float32),
    )
    shared = (
        lax.psum_scatter(grad_router, ("dp", "expert"), scatter_dimension=0, tiled=True),
        lax.psum_scatter(grad_gain_attn, ("dp", "expert"), scatter_dimension=0, tiled=True),
        lax.psum_scatter(grad_gain_mlp, ("dp", "expert"), scatter_dimension=0, tiled=True),
    )
    return (
        output,
        grad_inputs,
        summed[0],
        summed[1],
        shared[0],
        shared[1],
        shared[2],
        summed[2][0, 0],
        summed[2][0, 1],
        summed[3],
        summed[4],
    )


def solution(mesh):
    placed = (
        P(("dp", "expert"), None),
        P(("dp", "expert"), None),
        P(("dp", "expert"), None),
        P(("dp", "expert"), None),
        P(("dp", "expert"), None),
        P(("dp", "expert"), None),
        P(("dp", "expert"), None),
        P(("dp", "expert")),
        P(("dp", "expert")),
        P(("dp", "expert")),
        P(("dp", "expert")),
        P("expert", None, None),
        P("expert", None, None),
    )
    return jax.shard_map(
        on_device,
        mesh=mesh,
        in_specs=placed,
        out_specs=(
            P(("dp", "expert"), None),
            P(("dp", "expert"), None),
            P("dp", None, "expert"),
            P("expert", "dp"),
            P(("dp", "expert"), None),
            P(("dp", "expert")),
            P(("dp", "expert")),
            P("expert"),
            P("expert"),
            P("expert", "dp", None),
            P("expert", "dp", None),
        ),
        check_vma=False,
    )
```

profile of v0, /device:TPU:0, one launch (start us, length us, event | category | flops | bytes accessed | tf_op | source)
XLA Modules:
  0.0 2162.2 jit_solution(9898101751853634901)
XLA Ops:
  12.1 43.5 %all-reduce.8 = (bf16[2048]{0:T(1024)(128)(2,1)S(1)}, bf16[2048]{0:T(1024)(128)(2,1)S(1)}, bf16[2048]{0:T(1024)(128)(2,1)S(1)}, bf16[2048]{0:T(1024)(128)(2,1)S(1)}) all-reduce(bf16[2048]{0:T(1024)(128)(2,1)S(1)} %dynamic-update-slice, bf16[2048]{0:T(1024)(128)(2,1)S(1)} %dynamic-update-slice.2, ...), channel_id=1, replica_groups=mesh['dp'=4,'expert'=8] {'dp','expert'}, use_global_device_ids=true, to_apply=%add | all-reduce | flops 8192 | bytes 32768
  55.7 41.7 %all-gather = bf16[32,64,24]{1,2,0:T(8,128)(2,1)S(1)} all-gather(bf16[1,64,24]{1,2,0:T(8,128)(2,1)} %bitcast.186), channel_id=1, replica_groups=mesh['dp'=4,'expert'=8] {'dp','expert'}, dimensions={0}, use_global_device_ids=true | all-gather | bytes 101376 | tf_op jit(solution)/shard_map/all_gather | solution.py:84
  100.0 71.0 %all-gather.4.cloned.1.call-done = bf16[2048,6144]{1,0:T(8,128)(2,1)} async-done(((bf16[64,6144]{1,0:T(8,128)(2,1)}), bf16[2048,6144]{1,0:T(8,128)(2,1)}) %all-gather.4.cloned.1.call-update) | async-done | bytes 25165840 | tf_op jit(solution)/shard_map/all_gather | solution.py:82
  171.0 11.2 fusion.59
  191.8 57.7 %all-gather.6.cloned.1.call-done = bf16[2048,2048]{1,0:T(8,128)(2,1)} async-done(((bf16[64,2048]{1,0:T(8,128)(2,1)}), bf16[2048,2048]{1,0:T(8,128)(2,1)}) %all-gather.6.cloned.1.call-update) | async-done | bytes 8388624 | tf_op jit(solution)/shard_map/all_gather | solution.py:83
  256.8 19.1 fusion.2
  278.0 159.0 %all_to_all.66 = bf16[24,72,2048]{2,1,0:T(8,128)(2,1)S(1)} all-to-all(bf16[24,72,2048]{2,1,0:T(8,128)(2,1)S(1)} %bitcast.163), channel_id=1, replica_groups=mesh['dp'=4,'expert'=8] {'expert'}, dimensions={0} | all-to-all | bytes 14155776 | tf_op jit(solution)/shard_map/all_to_all | solution.py:150
  440.6 24.6 %fusion.85 = f32[3,576,2048]{2,1,0:T(8,128)} fusion(bf16[3,576,2048]{2,1,0:T(8,128)(2,1)} %bitcast.160, bf16[3,2048,2048]{2,1,0:T(8,128)(2,1)} %param.24), kind=kOutput, calls=%fused_computation.172 | convolution fusion | flops 14495514624 | bytes 46399488 | tf_op jit(solution)/shard_map/erd,edf->erf/dot_general | solution.py:151
  471.6 13.9 convolution_convert_fusion.6
  485.5 22.9 %copy.145 = bf16[3,576,2048]{2,0,1:T(4,128)(2,1)} copy(bf16[3,576,2048]{2,1,0:T(8,128)(2,1)S(1)} %convolution_convert_fusion.6) | data formatting | bytes 14155776 | tf_op jit(solution)/shard_map/convert_element_type | solution.py:160
  514.7 205.7 %all-to-all-done.1 = bf16[3,576,2048]{2,0,1:T(4,128)(2,1)} async-done(((bf16[3,576,2048]{2,0,1:T(4,128)(2,1)}), bf16[3,576,2048]{2,0,1:T(4,128)(2,1)}, u32[]{:S(2)}, u32[]{:S(2)}) %all-to-all-start.1) | async-done | bytes 7077920 | tf_op jit(solution)/shard_map/all_to_all | solution.py:161
  720.4 11.9 copy.146
  732.2 16.6 gather_fusion
  754.1 14.3 scatter_custom_fusion
  768.3 159.7 %all_to_all.67 = bf16[24,72,2048]{2,1,0:T(8,128)(2,1)S(1)} all-to-all(bf16[24,72,2048]{2,1,0:T(8,128)(2,1)} %bitcast.166), channel_id=1, replica_groups=mesh['dp'=4,'expert'=8] {'expert'}, dimensions={0} | all-to-all | bytes 14155776 | tf_op jit(solution)/shard_map/all_to_all | solution.py:180
  931.8 22.4 %multiply_convert_fusion.1 = (bf16[3,576,1024]{2,1,0:T(8,128)(2,1)}, bf16[3,576,1024]{2,1,0:T(8,128)(2,1)}) fusion(f32[3,576,2048]{2,1,0:T(8,128)} %fusion.85, bf16[3,576,2048]{2,1,0:T(8,128)(2,1)} %bitcast.176, bf16[3,1024,2048]{2,1,0:T(8,128)(2,1)} %param.25), kind=kOutput, calls=%fused_computation.15 | convolution fusion | flops 7270760448 | bytes 40894464 | tf_op jit(solution)/shard_map/erd,efd->erf/dot_general | solution.py:181
  954.1 21.6 convolution_convert_fusion.5
  975.7 11.5 copy.150
  1001.5 197.3 %all-to-all-done.3 = bf16[3,576,2048]{2,0,1:T(4,128)(2,1)} async-done(((bf16[3,576,2048]{2,0,1:T(4,128)(2,1)}), bf16[3,576,2048]{2,0,1:T(4,128)(2,1)}, u32[]{:S(2)}, u32[]{:S(2)}) %all-to-all-start.3) | async-done | bytes 7077920 | tf_op jit(solution)/shard_map/all_to_all | solution.py:196
  1247.5 13.5 convolution_convert_fusion
  1261.0 32.6 %copy.163 = bf16[2048,6144]{0,1:T(8,128)(2,1)} copy(bf16[2048,6144]{1,0:T(8,128)(2,1)} %convolution_convert_fusion) | data formatting | bytes 50331648 | tf_op jit(solution)/shard_map/convert_element_type | solution.py:249
  1297.5 16.6 convolution_convert_fusion.4
  1315.2 26.6 %convolution_convert_fusion.1 = bf16[3,2048,2048]{2,1,0:T(8,128)(2,1)} fusion(bf16[3,576,2048]{2,1,0:T(8,128)(2,1)} %bitcast.161, bf16[3,576,1024]{2,1,0:T(8,128)(2,1)} %get-tuple-element.80, bf16[3,576,1024]{2,1,0:T(8,128)(2,1)} %get-tuple-element.79), kind=kOutput, calls=%fused_computation.5 | convolution fusion | flops 14522253312 | bytes 39321600 | tf_op jit(solution)/shard_map/erd,erf->edf/dot_general | solution.py:190
  1341.9 218.4 %reduce-scatter.13.cloned.1.call-done = bf16[2048,3,256]{0,2,1:T(8,128)(2,1)} async-done(((bf16[2048,3,2048]{0,2,1:T(8,128)(2,1)}), bf16[2048,3,256]{0,2,1:T(8,128)(2,1)}) %reduce-scatter.13.cloned.1.call-update) | async-done | bytes 3145744 | tf_op jit(solution)/shard_map/reduce_scatter | solution.py:248
  1560.9 135.3 %reduce-scatter.25.cloned.1.call-done = f32[64,24]{1,0:T(8,128)} async-done(((f32[2048,24]{1,0:T(8,128)}), f32[64,24]{1,0:T(8,128)}) %reduce-scatter.25.cloned.1.call-update) | async-done | bytes 6160
  1697.6 14.9 fusion.20
  1712.5 37.2 %all-reduce.7 = (f32[2048]{0:T(1024)S(1)}, f32[2048]{0:T(1024)S(1)}) all-reduce(f32[2048]{0:T(1024)S(1)} %get-tuple-element.65, f32[2048]{0:T(1024)S(1)} %get-tuple-element.63), channel_id=7, replica_groups=mesh['dp'=4,'expert'=8] {'dp','expert'}, use_global_device_ids=true, to_apply=%region_28.29.clone | all-reduce | flops 4096 | bytes 32768
  1755.0 9.9 all-reduce.6
  1766.1 83.5 %reduce-scatter.23.cloned.1.call-done = bf16[3,256,2048]{2,1,0:T(8,128)(2,1)} async-done(((bf16[3,1024,2048]{2,1,0:T(8,128)(2,1)}), bf16[3,256,2048]{2,1,0:T(8,128)(2,1)}) %reduce-scatter.23.cloned.1.call-update) | async-done | bytes 3145744 | tf_op jit(solution)/shard_map/reduce_scatter | solution.py:272
  1855.0 25.2 %reduce-scatter.19.cloned.1.call-done = bf16[256,512]{1,0:T(8,128)(2,1)} async-done(((bf16[256,2048]{1,0:T(8,128)(2,1)}), bf16[256,512]{1,0:T(8,128)(2,1)}) %reduce-scatter.19.cloned.1.call-update) | async-done | bytes 262160 | tf_op jit(solution)/shard_map/reduce_scatter | solution.py:263
  1882.0 223.5 %reduce-scatter.21.cloned.1.call-done = bf16[3,512,2048]{2,1,0:T(8,128)(2,1)} async-done(((bf16[3,2048,2048]{2,1,0:T(8,128)(2,1)}), bf16[3,512,2048]{2,1,0:T(8,128)(2,1)}) %reduce-scatter.21.cloned.1.call-update) | async-done | bytes 6291472 | tf_op jit(solution)/shard_map/reduce_scatter | solution.py:269
  2114.6 37.7 %reduce-scatter.15.cloned.1.call-done = bf16[512,3,256]{0,2,1:T(8,128)(2,1)} async-done(((bf16[2048,3,256]{0,2,1:T(8,128)(2,1)}), bf16[512,3,256]{0,2,1:T(8,128)(2,1)}) %reduce-scatter.15.cloned.1.call-update) | async-done | bytes 786448 | tf_op jit(solution)/shard_map/reduce_scatter | solution.py:260
  (242 shorter events, 146.2 us)
Async XLA Ops:
  7.2 91.3 %copy-start.7 = (bf16[192,2048]{1,0:T(8,128)(2,1)S(1)}, bf16[192,2048]{1,0:T(8,128)(2,1)}, u32[]{:S(2)}) copy-start(bf16[192,2048]{1,0:T(8,128)(2,1)} %param.13) | copy-start | bytes 2359300
  7.2 91.7 %copy-start.52 = (s32[1,192]{1,0:T(1,128)S(1)}, s32[1,192]{1,0:T(1,128)}, u32[]{:S(2)}) copy-start(s32[1,192]{1,0:T(1,128)} %param.15) | copy-start | bytes 2308
  7.2 163.8 %all-gather.4.cloned.1.call-start = ((), (), s32[]{:S(2)}) async-start(), calls=%async_computation.12 | async-start | bytes 25952256 | tf_op jit(solution)/shard_map/all_gather | solution.py:82
  7.9 241.6 %all-gather.6.cloned.1.call-start = ((), (), s32[]{:S(2)}) async-start(), calls=%async_computation.13 | async-start | bytes 8650752 | tf_op jit(solution)/shard_map/all_gather | solution.py:83
  55.6 126.6 %copy-start.30 = (f32[2048]{0:T(1024)}, f32[2048]{0:T(1024)S(1)}, u32[]{:S(2)}) copy-start(f32[2048]{0:T(1024)S(1)} %convert_element_type.154) | copy-start | bytes 24580
  55.6 126.9 %copy-start.34 = (f32[2048]{0:T(1024)}, f32[2048]{0:T(1024)S(1)}, u32[]{:S(2)}) copy-start(f32[2048]{0:T(1024)S(1)} %convert_element_type.158) | copy-start | bytes 24580
  55.6 126.9 %copy-start.36 = (f32[2048]{0:T(1024)}, f32[2048]{0:T(1024)S(1)}, u32[]{:S(2)}) copy-start(f32[2048]{0:T(1024)S(1)} %convert_element_type.157) | copy-start | bytes 24580
  55.6 199.3 %copy-start.38 = (f32[2048]{0:T(1024)}, f32[2048]{0:T(1024)S(1)}, u32[]{:S(2)}) copy-start(f32[2048]{0:T(1024)S(1)} %convert_element_type.164) | copy-start | bytes 24580
  97.7 158.6 %copy-start.27 = (bf16[2048,24]{0,1:T(8,128)(2,1)}, bf16[2048,24]{0,1:T(8,128)(2,1)S(1)}, u32[]{:S(2)}) copy-start(bf16[2048,24]{0,1:T(8,128)(2,1)S(1)} %reshape.545) | copy-start | bytes 294916
  98.7 83.5 %copy-start.44 = (f32[192]{0:T(256)}, f32[192]{0:T(256)S(1)}, u32[]{:S(2)}) copy-start(f32[192]{0:T(256)S(1)} %add_rsqrt_fusion.3) | copy-start | bytes 2308
  100.0 84.9 %copy-start.25 = (f32[192,64]{1,0:T(8,128)}, f32[192,64]{1,0:T(8,128)S(1)}, u32[]{:S(2)}) copy-start(f32[192,64]{1,0:T(8,128)S(1)} %get-tuple-element.107) | copy-start | bytes 147460
  182.2 6.9 copy-start.2
  191.8 63.1 %copy-start.19 = (bf16[1,192,16,128]{3,2,1,0:T(8,128)(2,1)}, bf16[1,192,16,128]{3,2,1,0:T(8,128)(2,1)S(1)}, u32[]{:S(2)}) copy-start(bf16[1,192,16,128]{3,2,1,0:T(8,128)(2,1)S(1)} %copy.139) | copy-start | bytes 2359300
  256.3 21.7 %copy-start.5 = (bf16[192,2048]{1,0:T(8,128)(2,1)}, bf16[192,2048]{1,0:T(8,128)(2,1)S(1)}, u32[]{:S(2)}) copy-start(bf16[192,2048]{1,0:T(8,128)(2,1)S(1)} %multiply_convert_fusion.6) | copy-start | bytes 2359300
  471.5 13.9 copy-start.21
  508.4 5.6 copy-start.22
  508.4 212.0 %all-to-all-start.1 = ((bf16[3,576,2048]{2,0,1:T(4,128)(2,1)}), bf16[3,576,2048]{2,0,1:T(4,128)(2,1)}, u32[]{:S(2)}, u32[]{:S(2)}) async-start(bf16[3,576,2048]{2,0,1:T(4,128)(2,1)} %copy.145), calls=%async_computation.1 | async-start | bytes 18874368 | tf_op jit(solution)/shard_map/all_to_all | solution.py:161
  987.2 5.3 copy-start.41
  987.2 211.6 %all-to-all-start.3 = ((bf16[3,576,2048]{2,0,1:T(4,128)(2,1)}), bf16[3,576,2048]{2,0,1:T(4,128)(2,1)}, u32[]{:S(2)}, u32[]{:S(2)}) async-start(bf16[3,576,2048]{2,0,1:T(4,128)(2,1)} %copy.150), calls=%async_computation.3 | async-start | bytes 18874368 | tf_op jit(solution)/shard_map/all_to_all | solution.py:196
  992.5 321.7 %reduce-scatter.17.cloned.1.call-start = ((), (), s32[]{:S(2)}) async-start(), calls=%async_computation.16 | async-start | bytes 9437184 | tf_op jit(solution)/shard_map/reduce_scatter | solution.py:251
  1224.8 9.7 slice-start
  1224.8 335.5 %reduce-scatter.13.cloned.1.call-start = ((), (), s32[]{:S(2)}) async-start(), calls=%async_computation.14 | async-start | bytes 28311552 | tf_op jit(solution)/shard_map/reduce_scatter | solution.py:248
  1225.5 6.7 copy-start.1
  1225.6 8.9 slice-start.1
  1293.7 402.5 %reduce-scatter.25.cloned.1.call-start = ((), (), s32[]{:S(2)}) async-start(), calls=%async_computation.20 | async-start | bytes 1081344
  1296.3 457.8 %reduce-scatter.27.cloned.1.call-start = ((), (), s32[]{:S(2)}) async-start(), calls=%async_computation.21 | async-start | bytes 589824
  1297.5 552.1 %reduce-scatter.23.cloned.1.call-start = ((), (), s32[]{:S(2)}) async-start(), calls=%async_computation.19 | async-start | bytes 15728640 | tf_op jit(solution)/shard_map/reduce_scatter | solution.py:272
  1314.1 566.1 %reduce-scatter.19.cloned.1.call-start = ((), (), s32[]{:S(2)}) async-start(), calls=%async_computation.17 | async-start | bytes 1310720 | tf_op jit(solution)/shard_map/reduce_scatter | solution.py:263
  1314.9 790.7 %reduce-scatter.21.cloned.1.call-start = ((), (), s32[]{:S(2)}) async-start(), calls=%async_computation.18 | async-start | bytes 31457280 | tf_op jit(solution)/shard_map/reduce_scatter | solution.py:269
  1341.8 218.5 %copy-start.53 = (u32[32]{0:T(128)S(1)}, u32[32]{0:T(128)}, u32[]{:S(2)}) copy-start(u32[32]{0:T(128)} %constant.82) | copy-start | bytes 388
  1341.8 355.8 %copy-start.9 = (bf16[192,2048]{1,0:T(8,128)(2,1)S(1)}, bf16[192,2048]{1,0:T(8,128)(2,1)}, u32[]{:S(2)}) copy-start(bf16[192,2048]{1,0:T(8,128)(2,1)} %param.13) | copy-start | bytes 2359300
  1341.8 810.5 %reduce-scatter.15.cloned.1.call-start = ((), (), s32[]{:S(2)}) async-start(), calls=%async_computation.15 | async-start | bytes 3932160 | tf_op jit(solution)/shard_map/reduce_scatter | solution.py:260
  (36 other events, 63.9 us)
Sparse Core Ops, SparseCore 0:
  11.0 159.8 all-gather.3
  174.0 75.5 all-gather.5
  1225.0 87.5 reduce-scatter.16
  1314.7 245.5 reduce-scatter.12
  1563.0 133.1 reduce-scatter.24
  1699.0 27.1 reduce-scatter.26
  1729.8 119.7 reduce-scatter.22
  1852.5 27.6 reduce-scatter.18
  1883.6 221.8 reduce-scatter.20
  2108.4 43.9 reduce-scatter.14
where the time goes:
time: 2170 us; the launch traced here: 2160 us
  waiting for transfers between devices  1260 us (58%)
  blocking collectives  451 us (21%)
  matrix products  198 us (9%)
  local copies, waits for them, and re-layouts  140 us (6%)
  other arithmetic  88.1 us (4%)
    reduce_scatter x1, waiting for transfers between devices, on_device(): lax.psum_scatter(grad_w_gate_up.astype(jnp.bfloat16), 'dp', scatter_dimen...  224 us
    reduce_scatter x1, waiting for transfers between devices, on_device(): lax.psum_scatter(grad_w_qkv.astype(jnp.bfloat16), 'expert', scatter_dimen...  218 us
    all_to_all x1, waiting for transfers between devices, on_device(): lax.all_to_all(expert_out, 'expert', split_axis=1, concat_axis=0, tiled=T...  206 us
    all_to_all x1, waiting for transfers between devices, on_device(): lax.all_to_all(grad_rows, 'expert', split_axis=1, concat_axis=0, tiled=True)  197 us
    all_to_all x1, blocking collectives, on_device(): lax.all_to_all(back_send, 'expert', split_axis=0, concat_axis=1, tiled=True)  160 us
    all_to_all x1, blocking collectives, on_device(): lax.all_to_all(send_rows, 'expert', split_axis=0, concat_axis=1, tiled=True)  159 us
    unnamed x12, waiting for transfers between devices  137 us
    unnamed x3, blocking collectives  90.6 us
  transfers between devices with their start and end apart: 12, of which 10 were waited for; matrix products, arithmetic and copies ran while one was open for 9% of the time, Pallas kernels for 0%

commit v1 on v0

--- a/solution.py
+++ b/solution.py
@@ -158,8 +158,11 @@
     expert_out = jnp.einsum(
         "erf,efd->erd", activated, w_down, preferred_element_type=jnp.float32
     ).astype(jnp.bfloat16)
-    returned = lax.all_to_all(
-        expert_out, "expert", split_axis=1, concat_axis=0, tiled=True
+    returned = jnp.concatenate(
+        lax.all_to_all(
+            jnp.stack(jnp.split(expert_out, lax.axis_size("expert"), axis=1)), "expert", 0, 0
+        ),
+        axis=0,
     ).reshape(slot_count, model_dim)
     picked = (
         jnp.take(returned, slot_flat, axis=0)

time: 2170 us -> 2080 us (0.959)
  waiting for transfers between devices: 1260 us -> 1210 us
  local copies, waits for them, and re-layouts: 140 us -> 113 us
    all_to_all x1, waiting for transfers between devices: 206 us -> 155 us  [on_device(): lax.all_to_all(jnp.stack(jnp.split(expert_out, lax.axis_size('expert'), a...]
    convert_element_type x1 -> x0, local copies, waits for them, and re-layouts: 22.9 us -> none  [on_device(): expert_out = jnp.einsum('erf,efd->erd', activated, w_down, preferred_elem...]
where the time goes in v1:
time: 2080 us; the launch traced here: 2070 us
  waiting for transfers between devices  1210 us (58%)
  blocking collectives  451 us (22%)
  matrix products  198 us (10%)
  local copies, waits for them, and re-layouts  113 us (5%)
  other arithmetic  77.4 us (4%)
    reduce_scatter x1, waiting for transfers between devices, on_device(): lax.psum_scatter(grad_w_gate_up.astype(jnp.bfloat16), 'dp', scatter_dimen...  224 us
    reduce_scatter x1, waiting for transfers between devices, on_device(): lax.psum_scatter(grad_w_qkv.astype(jnp.bfloat16), 'expert', scatter_dimen...  219 us
    all_to_all x1, waiting for transfers between devices, on_device(): lax.all_to_all(grad_rows, 'expert', split_axis=1, concat_axis=0, tiled=True)  197 us
    all_to_all x1, blocking collectives, on_device(): lax.all_to_all(back_send, 'expert', split_axis=0, concat_axis=1, tiled=True)  160 us
    all_to_all x1, blocking collectives, on_device(): lax.all_to_all(send_rows, 'expert', split_axis=0, concat_axis=1, tiled=True)  159 us
    all_to_all x1, waiting for transfers between devices, on_device(): lax.all_to_all(jnp.stack(jnp.split(expert_out, lax.axis_size('expert'), a...  155 us
    unnamed x12, waiting for transfers between devices  137 us
    unnamed x3, blocking collectives  90.6 us
  transfers between devices with their start and end apart: 12, of which 10 were waited for; matrix products, arithmetic and copies ran while one was open for 9% of the time, Pallas kernels for 0%

profile of v1, /device:TPU:0, one launch (start us, length us, event | category | flops | bytes accessed | tf_op | source)
XLA Modules:
  0.0 2071.3 jit_solution(16608478920202302566)
XLA Ops:
  12.1 43.5 %all-reduce.8 = (bf16[2048]{0:T(1024)(128)(2,1)S(1)}, bf16[2048]{0:T(1024)(128)(2,1)S(1)}, bf16[2048]{0:T(1024)(128)(2,1)S(1)}, bf16[2048]{0:T(1024)(128)(2,1)S(1)}) all-reduce(bf16[2048]{0:T(1024)(128)(2,1)S(1)} %dynamic-update-slice, bf16[2048]{0:T(1024)(128)(2,1)S(1)} %dynamic-update-slice.2, ...), channel_id=1, replica_groups=mesh['dp'=4,'expert'=8] {'dp','expert'}, use_global_device_ids=true, to_apply=%add | all-reduce | flops 8192 | bytes 32768
  55.6 41.7 %all-gather = bf16[32,64,24]{1,2,0:T(8,128)(2,1)S(1)} all-gather(bf16[1,64,24]{1,2,0:T(8,128)(2,1)} %bitcast.214), channel_id=1, replica_groups=mesh['dp'=4,'expert'=8] {'dp','expert'}, dimensions={0}, use_global_device_ids=true | all-gather | bytes 101376 | tf_op jit(solution)/shard_map/all_gather | solution.py:84
  101.9 69.1 %all-gather.4.cloned.1.call-done = bf16[2048,6144]{1,0:T(8,128)(2,1)} async-done(((bf16[64,6144]{1,0:T(8,128)(2,1)}), bf16[2048,6144]{1,0:T(8,128)(2,1)}) %all-gather.4.cloned.1.call-update) | async-done | bytes 25165840 | tf_op jit(solution)/shard_map/all_gather | solution.py:82
  171.0 11.1 fusion.67
  191.6 57.9 %all-gather.6.cloned.1.call-done = bf16[2048,2048]{1,0:T(8,128)(2,1)} async-done(((bf16[64,2048]{1,0:T(8,128)(2,1)}), bf16[2048,2048]{1,0:T(8,128)(2,1)}) %all-gather.6.cloned.1.call-update) | async-done | bytes 8388624 | tf_op jit(solution)/shard_map/all_gather | solution.py:83
  265.6 159.0 %all_to_all.56 = bf16[24,72,2048]{2,1,0:T(8,128)(2,1)S(1)} all-to-all(bf16[24,72,2048]{2,1,0:T(8,128)(2,1)S(1)} %bitcast.191), channel_id=1, replica_groups=mesh['dp'=4,'expert'=8] {'expert'}, dimensions={0} | all-to-all | bytes 14155776 | tf_op jit(solution)/shard_map/all_to_all | solution.py:150
  428.2 24.3 %fusion.93 = f32[3,576,2048]{2,1,0:T(8,128)} fusion(bf16[3,576,2048]{2,1,0:T(8,128)(2,1)} %bitcast.188, bf16[3,2048,2048]{2,1,0:T(8,128)(2,1)} %param.24), kind=kOutput, calls=%fused_computation.188 | convolution fusion | flops 14495514624 | bytes 46399488 | tf_op jit(solution)/shard_map/erd,edf->erf/dot_general | solution.py:151
  458.8 13.9 convolution_convert_fusion.6
  486.3 155.1 %all-to-all-done.1 = bf16[8,3,72,2048]{3,2,1,0:T(8,128)(2,1)} async-done(((bf16[8,3,72,2048]{3,2,1,0:T(8,128)(2,1)}), bf16[8,3,72,2048]{3,2,1,0:T(8,128)(2,1)}, u32[]{:S(2)}, u32[]{:S(2)}) %all-to-all-start.1) | async-done | bytes 7077920 | tf_op jit(solution)/shard_map/all_to_all | solution.py:162
  641.5 16.6 gather_fusion
  663.3 14.1 scatter_custom_fusion
  677.4 159.9 %all_to_all.57 = bf16[24,72,2048]{2,1,0:T(8,128)(2,1)S(1)} all-to-all(bf16[24,72,2048]{2,1,0:T(8,128)(2,1)} %bitcast.194), channel_id=1, replica_groups=mesh['dp'=4,'expert'=8] {'expert'}, dimensions={0} | all-to-all | bytes 14155776 | tf_op jit(solution)/shard_map/all_to_all | solution.py:183
  841.0 22.3 %multiply_convert_fusion.1 = (bf16[3,576,1024]{2,1,0:T(8,128)(2,1)}, bf16[3,576,1024]{2,1,0:T(8,128)(2,1)}) fusion(f32[3,576,2048]{2,1,0:T(8,128)} %fusion.93, bf16[3,576,2048]{2,1,0:T(8,128)(2,1)} %bitcast.204, bf16[3,1024,2048]{2,1,0:T(8,128)(2,1)} %param.25), kind=kOutput, calls=%fused_computation.15 | convolution fusion | flops 7270760448 | bytes 40894464 | tf_op jit(solution)/shard_map/erd,efd->erf/dot_general | solution.py:184
  863.4 21.6 %convolution_convert_fusion.5 = bf16[3,576,2048]{2,1,0:T(8,128)(2,1)} fusion(bf16[3,2048,2048]{2,1,0:T(8,128)(2,1)} %param.24, bf16[3,576,1024]{2,1,0:T(8,128)(2,1)} %get-tuple-element.80, bf16[3,576,1024]{2,1,0:T(8,128)(2,1)} %get-tuple-element.79), kind=kOutput, calls=%fused_computation.24 | convolution fusion | flops 14513209344 | bytes 39321600 | tf_op jit(solution)/shard_map/erf,edf->erd/dot_general | solution.py:196
  885.0 11.5 copy.142
  901.9 8.9 multiply_reduce_fusion
  910.8 197.3 %all-to-all-done.3 = bf16[3,576,2048]{2,0,1:T(4,128)(2,1)} async-done(((bf16[3,576,2048]{2,0,1:T(4,128)(2,1)}), bf16[3,576,2048]{2,0,1:T(4,128)(2,1)}, u32[]{:S(2)}, u32[]{:S(2)}) %all-to-all-start.3) | async-done | bytes 7077920 | tf_op jit(solution)/shard_map/all_to_all | solution.py:199
  1108.1 8.8 copy.143
  1156.8 13.5 convolution_convert_fusion
  1170.3 32.4 %copy.155 = bf16[2048,6144]{0,1:T(8,128)(2,1)} copy(bf16[2048,6144]{1,0:T(8,128)(2,1)} %convolution_convert_fusion) | data formatting | bytes 50331648 | tf_op jit(solution)/shard_map/convert_element_type | solution.py:252
  1206.6 16.6 convolution_convert_fusion.4
  1224.2 26.6 %convolution_convert_fusion.1 = bf16[3,2048,2048]{2,1,0:T(8,128)(2,1)} fusion(bf16[3,576,2048]{2,1,0:T(8,128)(2,1)} %bitcast.189, bf16[3,576,1024]{2,1,0:T(8,128)(2,1)} %get-tuple-element.80, bf16[3,576,1024]{2,1,0:T(8,128)(2,1)} %get-tuple-element.79), kind=kOutput, calls=%fused_computation.5 | convolution fusion | flops 14522253312 | bytes 39321600 | tf_op jit(solution)/shard_map/erd,erf->edf/dot_general | solution.py:193
  1250.9 218.6 %reduce-scatter.13.cloned.1.call-done = bf16[2048,3,256]{0,2,1:T(8,128)(2,1)} async-done(((bf16[2048,3,2048]{0,2,1:T(8,128)(2,1)}), bf16[2048,3,256]{0,2,1:T(8,128)(2,1)}) %reduce-scatter.13.cloned.1.call-update) | async-done | bytes 3145744 | tf_op jit(solution)/shard_map/reduce_scatter | solution.py:251
  1470.2 135.2 %reduce-scatter.25.cloned.1.call-done = f32[64,24]{1,0:T(8,128)} async-done(((f32[2048,24]{1,0:T(8,128)}), f32[64,24]{1,0:T(8,128)}) %reduce-scatter.25.cloned.1.call-update) | async-done | bytes 6160
  1606.8 14.8 fusion.20
  1621.7 37.2 %all-reduce.7 = (f32[2048]{0:T(1024)S(1)}, f32[2048]{0:T(1024)S(1)}) all-reduce(f32[2048]{0:T(1024)S(1)} %get-tuple-element.65, f32[2048]{0:T(1024)S(1)} %get-tuple-element.63), channel_id=7, replica_groups=mesh['dp'=4,'expert'=8] {'dp','expert'}, use_global_device_ids=true, to_apply=%region_28.29.clone | all-reduce | flops 4096 | bytes 32768
  1664.2 9.8 all-reduce.6
  1675.3 83.5 %reduce-scatter.23.cloned.1.call-done = bf16[3,256,2048]{2,1,0:T(8,128)(2,1)} async-done(((bf16[3,1024,2048]{2,1,0:T(8,128)(2,1)}), bf16[3,256,2048]{2,1,0:T(8,128)(2,1)}) %reduce-scatter.23.cloned.1.call-update) | async-done | bytes 3145744 | tf_op jit(solution)/shard_map/reduce_scatter | solution.py:275
  1764.2 25.2 %reduce-scatter.19.cloned.1.call-done = bf16[256,512]{1,0:T(8,128)(2,1)} async-done(((bf16[256,2048]{1,0:T(8,128)(2,1)}), bf16[256,512]{1,0:T(8,128)(2,1)}) %reduce-scatter.19.cloned.1.call-update) | async-done | bytes 262160 | tf_op jit(solution)/shard_map/reduce_scatter | solution.py:266
  1791.2 223.5 %reduce-scatter.21.cloned.1.call-done = bf16[3,512,2048]{2,1,0:T(8,128)(2,1)} async-done(((bf16[3,2048,2048]{2,1,0:T(8,128)(2,1)}), bf16[3,512,2048]{2,1,0:T(8,128)(2,1)}) %reduce-scatter.21.cloned.1.call-update) | async-done | bytes 6291472 | tf_op jit(solution)/shard_map/reduce_scatter | solution.py:272
  2014.7 9.1 convert_element_type.190
  2023.8 37.7 %reduce-scatter.15.cloned.1.call-done = bf16[512,3,256]{0,2,1:T(8,128)(2,1)} async-done(((bf16[2048,3,256]{0,2,1:T(8,128)(2,1)}), bf16[512,3,256]{0,2,1:T(8,128)(2,1)}) %reduce-scatter.15.cloned.1.call-update) | async-done | bytes 786448 | tf_op jit(solution)/shard_map/reduce_scatter | solution.py:263
  (246 shorter events, 135.1 us)
Async XLA Ops:
  7.2 163.8 %copy-start.7 = (bf16[192,2048]{1,0:T(8,128)(2,1)S(1)}, bf16[192,2048]{1,0:T(8,128)(2,1)}, u32[]{:S(2)}) copy-start(bf16[192,2048]{1,0:T(8,128)(2,1)} %param.13) | copy-start | bytes 2359300
  7.2 163.8 %all-gather.4.cloned.1.call-start = ((), (), s32[]{:S(2)}) async-start(), calls=%async_computation.12 | async-start | bytes 25952256 | tf_op jit(solution)/shard_map/all_gather | solution.py:82
  7.9 241.6 %all-gather.6.cloned.1.call-start = ((), (), s32[]{:S(2)}) async-start(), calls=%async_computation.13 | async-start | bytes 8650752 | tf_op jit(solution)/shard_map/all_gather | solution.py:83
  55.6 126.5 %copy-start.30 = (f32[2048]{0:T(1024)}, f32[2048]{0:T(1024)S(1)}, u32[]{:S(2)}) copy-start(f32[2048]{0:T(1024)S(1)} %convert_element_type.154) | copy-start | bytes 24580
  55.6 126.8 %copy-start.34 = (f32[2048]{0:T(1024)}, f32[2048]{0:T(1024)S(1)}, u32[]{:S(2)}) copy-start(f32[2048]{0:T(1024)S(1)} %convert_element_type.158) | copy-start | bytes 24580
  55.6 126.8 %copy-start.36 = (f32[2048]{0:T(1024)}, f32[2048]{0:T(1024)S(1)}, u32[]{:S(2)}) copy-start(f32[2048]{0:T(1024)S(1)} %convert_element_type.157) | copy-start | bytes 24580
  55.6 199.3 %copy-start.38 = (f32[2048]{0:T(1024)}, f32[2048]{0:T(1024)S(1)}, u32[]{:S(2)}) copy-start(f32[2048]{0:T(1024)S(1)} %convert_element_type.164) | copy-start | bytes 24580
  97.6 158.6 %copy-start.27 = (bf16[2048,24]{0,1:T(8,128)(2,1)}, bf16[2048,24]{0,1:T(8,128)(2,1)S(1)}, u32[]{:S(2)}) copy-start(bf16[2048,24]{0,1:T(8,128)(2,1)S(1)} %reshape.540) | copy-start | bytes 294916
  99.8 82.3 %copy-start.44 = (f32[192]{0:T(256)}, f32[192]{0:T(256)S(1)}, u32[]{:S(2)}) copy-start(f32[192]{0:T(256)S(1)} %add_rsqrt_fusion.3) | copy-start | bytes 2308
  101.9 83.0 %copy-start.25 = (f32[192,64]{1,0:T(8,128)}, f32[192,64]{1,0:T(8,128)S(1)}, u32[]{:S(2)}) copy-start(f32[192,64]{1,0:T(8,128)S(1)} %get-tuple-element.107) | copy-start | bytes 147460
  182.1 6.9 copy-start.2
  191.6 63.3 %copy-start.19 = (bf16[1,192,16,128]{3,2,1,0:T(8,128)(2,1)}, bf16[1,192,16,128]{3,2,1,0:T(8,128)(2,1)S(1)}, u32[]{:S(2)}) copy-start(bf16[1,192,16,128]{3,2,1,0:T(8,128)(2,1)S(1)} %copy.133) | copy-start | bytes 2359300
  256.2 9.4 copy-start.5
  458.8 14.0 copy-start.21
  480.6 5.1 copy-start.22
  480.6 160.9 %all-to-all-start.1 = ((bf16[8,3,72,2048]{3,2,1,0:T(8,128)(2,1)}), bf16[8,3,72,2048]{3,2,1,0:T(8,128)(2,1)}, u32[]{:S(2)}, u32[]{:S(2)}) async-start(bf16[8,3,72,2048]{3,2,1,0:T(8,128)(2,1)} %fusion.38), calls=%async_computation.1 | async-start | bytes 14155776 | tf_op jit(solution)/shard_map/all_to_all | solution.py:162
  896.5 5.3 copy-start.41
  896.5 211.6 %all-to-all-start.3 = ((bf16[3,576,2048]{2,0,1:T(4,128)(2,1)}), bf16[3,576,2048]{2,0,1:T(4,128)(2,1)}, u32[]{:S(2)}, u32[]{:S(2)}) async-start(bf16[3,576,2048]{2,0,1:T(4,128)(2,1)} %copy.142), calls=%async_computation.3 | async-start | bytes 18874368 | tf_op jit(solution)/shard_map/all_to_all | solution.py:199
  901.8 321.4 %reduce-scatter.17.cloned.1.call-start = ((), (), s32[]{:S(2)}) async-start(), calls=%async_computation.16 | async-start | bytes 9437184 | tf_op jit(solution)/shard_map/reduce_scatter | solution.py:254
  1120.8 4.8 copy-start.47
  1134.1 9.7 slice-start
  1134.1 335.4 %reduce-scatter.13.cloned.1.call-start = ((), (), s32[]{:S(2)}) async-start(), calls=%async_computation.14 | async-start | bytes 28311552 | tf_op jit(solution)/shard_map/reduce_scatter | solution.py:251
  1134.8 6.7 copy-start.1
  1134.8 8.9 slice-start.1
  1202.7 402.7 %reduce-scatter.25.cloned.1.call-start = ((), (), s32[]{:S(2)}) async-start(), calls=%async_computation.20 | async-start | bytes 1081344
  1205.3 458.0 %reduce-scatter.27.cloned.1.call-start = ((), (), s32[]{:S(2)}) async-start(), calls=%async_computation.21 | async-start | bytes 589824
  1206.5 552.3 %reduce-scatter.23.cloned.1.call-start = ((), (), s32[]{:S(2)}) async-start(), calls=%async_computation.19 | async-start | bytes 15728640 | tf_op jit(solution)/shard_map/reduce_scatter | solution.py:275
  1223.1 566.2 %reduce-scatter.19.cloned.1.call-start = ((), (), s32[]{:S(2)}) async-start(), calls=%async_computation.17 | async-start | bytes 1310720 | tf_op jit(solution)/shard_map/reduce_scatter | solution.py:266
  1223.9 790.8 %reduce-scatter.21.cloned.1.call-start = ((), (), s32[]{:S(2)}) async-start(), calls=%async_computation.18 | async-start | bytes 31457280 | tf_op jit(solution)/shard_map/reduce_scatter | solution.py:272
  1250.9 218.7 %copy-start.52 = (u32[32]{0:T(128)S(1)}, u32[32]{0:T(128)}, u32[]{:S(2)}) copy-start(u32[32]{0:T(128)} %constant.82) | copy-start | bytes 388
  1250.9 355.9 %copy-start.9 = (bf16[192,2048]{1,0:T(8,128)(2,1)S(1)}, bf16[192,2048]{1,0:T(8,128)(2,1)}, u32[]{:S(2)}) copy-start(bf16[192,2048]{1,0:T(8,128)(2,1)} %param.13) | copy-start | bytes 2359300
  1250.9 810.6 %reduce-scatter.15.cloned.1.call-start = ((), (), s32[]{:S(2)}) async-start(), calls=%async_computation.15 | async-start | bytes 3932160 | tf_op jit(solution)/shard_map/reduce_scatter | solution.py:263
  (35 other events, 60.8 us)
Sparse Core Ops, SparseCore 0:
  11.0 159.8 all-gather.3
  173.9 75.5 all-gather.5
  1134.2 87.4 reduce-scatter.16
  1224.0 245.5 reduce-scatter.12
  1472.2 133.1 reduce-scatter.24
  1608.2 27.2 reduce-scatter.26
  1639.1 119.6 reduce-scatter.22
  1761.7 27.6 reduce-scatter.18
  1792.8 221.8 reduce-scatter.20
  2017.5 43.9 reduce-scatter.14
